TPU v7x, 32 devices: a whole 2x2x4 slice. The times are simulated.
32 devices in a mesh: dp: 8 (over z, x), seq: 4 (over y, core).
Axes of the slice: x: 2, y: 2, z: 4, core: 2. Of those that a mesh axis runs over, the one named last changes fastest.
Arguments:
- enc_rows: bfloat16 [32, 256, 1280], P('dp', 'seq'), may hold values from -100 to 100
- out_weight: bfloat16 [1280, 512], replicated, may hold values from -3 to 3
- labels: int32 [32, 63], P('dp'), may hold values from 1 to 511
- label_count: int32 [32], P('dp'), may hold values from 1 to 63, as said below
- frame_count: int32 [32], P('dp'), may hold values from 128 to 256, as said below
Outputs:
- logit_grad: bfloat16 [32, 256, 512], P('dp', 'seq')
- row_grad: bfloat16 [32, 256, 1280], P('dp', 'seq')
- weight_grad: float32 [1280, 512], P('dp', 'seq')
Inputs may be any that keep to these rules, and one draw needn't show every extreme that they name: `labels`: character ids; id 0 is the blank and never appears. `label_count`: some utterance has 63 labels in every draw. `frame_count`: some utterance has 256 frames in every draw.
All inputs are finite; a program needn't handle non-finite values.
Results may differ from a plain program's by a relative error of at most 0.0043.
Values sent between devices are 32-bit elements; how exact they have to be, the bound alone decides.
A program may use at most 64 MiB of HBM per device.

v0:
```python
import functools

import jax
import jax.numpy as jnp
from jax import lax
from jax.experimental import pallas as pl
from jax.experimental.pallas import tpu as pltpu
from jax.sharding import PartitionSpec as P

negative_fill = -1e30
LANES = 128
SPLIT = 4
UNROLL = 32
MESH = pl.DeviceIdType.MESH
BOTH_LAST = (((1,), (1,)), ((), ()))


def three_parts(values):
    high = values.astype(jnp.bfloat16)
    rest = values - high.astype(jnp.float32)
    middle = rest.astype(jnp.bfloat16)
    low = (rest - middle.astype(jnp.float32)).astype(jnp.bfloat16)
    return high, middle, low


def label_table(labels_ref, table_ref):
    utterances, length = labels_ref.shape
    table_ref[...] = jnp.zeros_like(table_ref)
    table_ref[0:utterances, 0:length] = labels_ref[...]
    table_ref[utterances:2 * utterances, 0:length] = labels_ref[...]
    return table_ref[...]


def share_emissions(seq_count, enc_ref, weight_ref, labels_ref,
                    logprob_ref, gathered_ref, table_ref, send_sems, recv_sems, before_sending):
    utterances, length = labels_ref.shape
    me = lax.axis_index("seq")
    frames = enc_ref.shape[0] // utterances
    vocabulary = weight_ref.shape[1]
    groups = gathered_ref.shape[1]
    pack = utterances // groups
    logits = jnp.dot(enc_ref[...], weight_ref[...], preferred_element_type=jnp.float32)
    highest = jnp.max(logits, axis=1, keepdims=True)
    total = jnp.sum(jnp.exp(logits - highest), axis=1, keepdims=True)
    logprob = logits - (highest + jnp.log(total))
    rows = lax.broadcasted_iota(jnp.int32, (vocabulary, LANES), 0)
    table = label_table(labels_ref, table_ref)
    lane = lax.broadcasted_iota(jnp.int32, table.shape, 1)
    for group in range(groups):
        picked = jnp.zeros((frames, LANES), jnp.float32)
        for inner in range(pack):
            utterance = group * pack + inner
            begin = inner * (length + 1)
            placed = pltpu.roll(table, begin, 1) if begin else table
            inside = (lane >= begin) & (lane <= begin + length)
            placed = jnp.where(inside, placed, -1)
            one_hot = jnp.where(
                rows == placed[utterance:utterance + 1, :], 1.0, 0.0
            ).astype(jnp.bfloat16)
            mine = logprob[utterance * frames:(utterance + 1) * frames]
            for part in three_parts(mine):
                picked += jnp.dot(part, one_hot, preferred_element_type=jnp.float32)
        gathered_ref[me, group] = picked
    logprob_ref[...] = logprob
    before_sending()
    copies = []
    for step in range(1, seq_count):
        peer = lax.rem(me + step, seq_count)
        copy = pltpu.make_async_remote_copy(
            src_ref=gathered_ref.at[me],
            dst_ref=gathered_ref.at[me],
            send_sem=send_sems.at[step - 1],
            recv_sem=recv_sems.at[step - 1],
            device_id={"seq": peer},
            device_id_type=MESH,
        )
        copy.start()
        copies.append(copy)
    for copy in copies:
        copy.wait()


def take_lanes(values, index):
    return jnp.take_along_axis(values, index, axis=1)


def spread(count_ref, utterance):
    values = jnp.full(utterance.shape, count_ref[0], jnp.int32)
    for u in range(1, count_ref.shape[0]):
        values = jnp.where(utterance == u, count_ref[u], values)
    return values


def lattice_gradients(label_count_ref, frame_count_ref, gathered_ref, labels_ref, logprob_ref,
                      logit_ref, table_ref, level_ref, factor_ref, mass_ref):
    utterances, length = labels_ref.shape
    seq_count, groups, frames = gathered_ref.shape[:3]
    steps = seq_count * frames
    rows = 2 * utterances
    slots = length + 1
    pack = utterances // groups
    span = LANES * SPLIT
    shape = (rows, LANES)
    row = lax.broadcasted_iota(jnp.int32, shape, 0)
    lane = lax.broadcasted_iota(jnp.int32, shape, 1)
    forward = row < utterances
    utterance = lax.rem(row, utterances)
    offset = lax.rem(utterance, pack) * slots
    label_rows = label_table(labels_ref, table_ref)
    label_count = spread(label_count_ref, utterance)
    frame_count = spread(frame_count_ref, utterance)
    first_usable = jnp.where(forward, 0, steps - frame_count)

    label_index, label_fill, jump_fill, label_start = [], [], [], []
    blank_fill, blank_start, label_chars = [], [], []
    for r in range(SPLIT):
        place = lane * SPLIT + r
        j = jnp.where(forward, place, span - 1 - place)
        real = j < length
        label_index.append(offset + jnp.clip(j, 0, slots - 1))
        label_fill.append(jnp.where(real, 0.0, negative_fill))
        before = jnp.where(forward, j - 1, j + 1)
        here_char = take_lanes(label_rows, jnp.clip(j, 0, LANES - 1))
        before_char = take_lanes(label_rows, jnp.clip(before, 0, LANES - 1))
        can_jump = real & (before >= 0) & (before < length) & (here_char != before_char)
        jump_fill.append(jnp.where(can_jump, 0.0, negative_fill))
        label_chars.append(jnp.where(real, here_char, -1))
        label_begin = j == jnp.where(forward, 0, label_count - 1)
        label_start.append(jnp.where(label_begin, 0.0, negative_fill))
        blank = jnp.where(forward, j, lax.rem(j + 1, span))
        blank_fill.append(jnp.where(blank < slots, 0.0, negative_fill))
        blank_begin = blank == jnp.where(forward, 0, label_count)
        blank_start.append(jnp.where(blank_begin, 0.0, negative_fill))
    blank_index = offset + slots - 1
    row_group = utterance // pack

    def frame_row(group, step):
        block = step // frames
        inside = lax.rem(step, frames)
        return jnp.broadcast_to(gathered_ref[block, group, pl.ds(inside, 1), :], shape)

    def raw_emission(step):
        raw = None
        for group in range(groups):
            early = frame_row(group, step)
            late = frame_row(group, steps - 1 - step)
            both = jnp.where(forward, early, late)
            raw = both if raw is None else jnp.where(row_group == group, both, raw)
        return raw

    def one_step(step, state):
        labels_v, blanks_v, labels_x, blanks_x = state
        raw = raw_emission(step)
        blank_emission = take_lanes(raw, blank_index)
        usable = step >= first_usable
        next_labels_v, next_blanks_v, next_labels_x, next_blanks_x = [], [], [], []
        full_labels, full_blanks = [], []
        for r in range(SPLIT):
            full_labels.append(labels_v[r] + (take_lanes(raw, label_index[r]) + label_fill[r]))
            full_blanks.append(blanks_v[r] + (blank_emission + blank_fill[r]))
            level_ref[step, r] = jnp.where(forward, full_labels[r], labels_v[r])
            level_ref[step, SPLIT + r] = jnp.where(forward, full_blanks[r], blanks_v[r])
            factor_ref[step, r] = labels_x[r]
            factor_ref[step, SPLIT + r] = blanks_x[r]
        for r in range(SPLIT):
            if r == 0:
                behind_v = pltpu.roll(full_labels[SPLIT - 1], 1, 1)
                behind_x = pltpu.roll(labels_x[SPLIT - 1], 1, 1)
            else:
                behind_v = full_labels[r - 1]
                behind_x = labels_x[r - 1]
            jump_v = behind_v + jump_fill[r]
            pivot = jnp.maximum(jnp.maximum(full_blanks[r], jump_v), full_labels[r])
            fresh_x = (
                jnp.exp(full_labels[r] - pivot) * labels_x[r]
                + jnp.exp(full_blanks[r] - pivot) * blanks_x[r]
                + jnp.exp(jump_v - pivot) * behind_x
            )
            next_labels_v.append(jnp.where(usable, pivot, label_start[r]))
            next_labels_x.append(jnp.where(usable, fresh_x, 1.0))
            pivot = jnp.maximum(full_blanks[r], behind_v)
            fresh_x = (
                jnp.exp(full_blanks[r] - pivot) * blanks_x[r]
                + jnp.exp(behind_v - pivot) * behind_x
            )
            next_blanks_v.append(jnp.where(usable, pivot, blank_start[r]))
            next_blanks_x.append(jnp.where(usable, fresh_x, 1.0))
        return (tuple(next_labels_v), tuple(next_blanks_v), tuple(next_labels_x), tuple(next_blanks_x))

    ones = (jnp.ones(shape, jnp.float32),) * SPLIT

    def run_block(block, state):
        labels_v, blanks_v = state
        full = (labels_v, blanks_v, ones, ones)
        for inner in range(UNROLL):
            full = one_step(block * UNROLL + inner, full)
        labels_v, blanks_v, labels_x, blanks_x = full
        labels_v = tuple(v + jnp.log(x) for v, x in zip(labels_v, labels_x))
        blanks_v = tuple(v + jnp.log(x) for v, x in zip(blanks_v, blanks_x))
        return labels_v, blanks_v

    lax.fori_loop(0, steps // UNROLL, run_block, (tuple(label_start), tuple(blank_start)))

    start = lax.axis_index("seq") * frames
    reverse = LANES - 1 - lane
    reverse_next = lax.rem(LANES - lane, LANES)
    chunk = 8

    def posterior_block(block, carry):
        for inner in range(chunk):
            frame = block * chunk + inner
            ahead = start + frame
            back = steps - 1 - ahead
            summed = []
            for r in range(SPLIT):
                other = SPLIT - 1 - r
                turned = take_lanes(level_ref[back, other] + jnp.log(factor_ref[back, other]), reverse)
                summed.append(
                    level_ref[ahead, r] + jnp.log(factor_ref[ahead, r])
                    + pltpu.roll(turned, utterances, 0)
                )
            for r in range(SPLIT):
                other = SPLIT + (SPLIT - r) % SPLIT
                turned = take_lanes(
                    level_ref[back, other] + jnp.log(factor_ref[back, other]),
                    reverse_next if r == 0 else reverse,
                )
                summed.append(
                    level_ref[ahead, SPLIT + r] + jnp.log(factor_ref[ahead, SPLIT + r])
                    + pltpu.roll(turned, utterances, 0)
                )
            highest = functools.reduce(jnp.maximum, summed)
            highest = jnp.max(highest, axis=1, keepdims=True)
            powers = [jnp.exp(term - highest) for term in summed]
            total = jnp.sum(sum(powers), axis=1, keepdims=True)
            scale = jnp.where(ahead < frame_count, 1.0, 0.0) / total
            for r in range(SPLIT):
                mass_ref[r, frame] = powers[r] * scale
            mass_ref[SPLIT, frame] = sum(powers[SPLIT:]) * scale
        return carry

    lax.fori_loop(0, frames // chunk, posterior_block, 0)

    vocabulary = logprob_ref.shape[1]
    chars = lax.broadcasted_iota(jnp.int32, (vocabulary, LANES), 0)
    columns = lax.broadcasted_iota(jnp.int32, (frames, vocabulary), 1)
    times = start + lax.broadcasted_iota(jnp.int32, (frames, vocabulary), 0)
    for u in range(utterances):
        mass = jnp.zeros((frames, vocabulary), jnp.float32)
        for r in range(SPLIT):
            one_hot = jnp.where(chars == label_chars[r][u:u + 1, :], 1.0, 0.0).astype(jnp.bfloat16)
            for part in three_parts(mass_ref[r, :, u, :])[:2]:
                mass += lax.dot_general(part, one_hot, BOTH_LAST, preferred_element_type=jnp.float32)
        blank_mass = jnp.sum(mass_ref[SPLIT, :, u, :], axis=1, keepdims=True)
        mass += jnp.where(columns == 0, blank_mass, 0.0)
        own = slice(u * frames, (u + 1) * frames)
        kept = jnp.where(times < frame_count_ref[u], jnp.exp(logprob_ref[own, :]) - mass, 0.0)
        logit_ref[own, :] = kept.astype(jnp.bfloat16)


def binary_digits(axis, count):
    index = lax.axis_index(axis)
    digits = []
    step = 1
    while step < count:
        digit = lax.rem(index // step, 2)
        digits.append((axis, digit, index + step * (1 - 2 * digit)))
        step *= 2
    return digits


def halving_plan(seq_count, dp_count):
    seq_bits = [("seq", i) for i in range(seq_count.bit_length() - 1)]
    dp_bits = [("dp", i) for i in range(dp_count.bit_length() - 1)]
    first, others = seq_bits[:1], seq_bits[1:]
    along = first + others + dp_bits
    across = first + dp_bits[:1] + others + dp_bits[1:]
    held = others[::-1] + dp_bits[::-1]
    return held, (along, across)


def row_chunks(rows):
    quarter = -(-rows // 10 // 8) * 8
    return [(low, min(quarter, rows - low)) for low in range(0, rows, quarter)]


def fused_kernel(seq_count, dp_count, label_count_ref, frame_count_ref, enc_ref, weight_ref,
                 labels_ref, logit_ref, row_ref, out_ref, logprob_ref, gathered_ref, table_ref,
                 level_ref, factor_ref, mass_ref, sent_ref, kept_ref, share_send, share_recv,
                 send_sems, recv_sems, *landed):
    me = lax.axis_index("seq")
    digits = {
        (axis, i): entry
        for axis, count in (("seq", seq_count), ("dp", dp_count))
        for i, entry in enumerate(binary_digits(axis, count))
    }
    greeted = [("seq", lax.rem(me + step, seq_count)) for step in range(1, seq_count)]
    greeted += [(axis, partner) for axis, _, partner in digits.values() if axis == "dp"]
    barrier = pltpu.get_barrier_semaphore()
    for axis, partner in greeted:
        pl.semaphore_signal(barrier, inc=1, device_id={axis: partner}, device_id_type=MESH)

    def before_sending():
        pl.semaphore_wait(barrier, len(greeted))

    share_emissions(seq_count, enc_ref, weight_ref, labels_ref, logprob_ref, gathered_ref,
                    table_ref, share_send, share_recv, before_sending)
    lattice_gradients(label_count_ref, frame_count_ref, gathered_ref, labels_ref, logprob_ref,
                      logit_ref, table_ref, level_ref, factor_ref, mass_ref)

    grad = logit_ref[...]
    columns = sent_ref.shape[-1]
    core = digits[("seq", 0)][1]
    even = [grad[:, s * columns:(s + 1) * columns] for s in range(0, seq_count, 2)]
    odd = [grad[:, s * columns:(s + 1) * columns] for s in range(1, seq_count, 2)]

    def fill(target_ref, halves):
        product = lax.dot_general(
            enc_ref[...], jnp.concatenate(halves, axis=1), (((0,), (0,)), ((), ())),
            preferred_element_type=jnp.float32,
        )
        high = (seq_count // 2).bit_length() - 1
        for h in range(seq_count // 2):
            place = tuple((h >> (high - 1 - i)) & 1 for i in range(high))
            piece = product[:, h * columns:(h + 1) * columns]
            target_ref[place] = piece.reshape(target_ref.shape[high:])

    first = core == 0
    fill(sent_ref, [jnp.where(first, o, e) for e, o in zip(even, odd)])

    held, orders = halving_plan(seq_count, dp_count)
    rows = out_ref.shape[0]
    chunks = row_chunks(rows)
    stages = len(held) + 1
    landing = [landed[c * stages:(c + 1) * stages] for c in range(len(chunks))]
    names = [list(held) for _ in chunks]
    pending = [None] * len(chunks)

    def dense(ref, low, size):
        return ref.at[(slice(None),) * len(held) + (pl.ds(low, size),)]

    def launch(c, stage, source, kept, bit):
        axis, _, partner = digits[bit]
        copy = pltpu.make_async_remote_copy(
            src_ref=source,
            dst_ref=landing[c][stage],
            send_sem=send_sems.at[c, stage],
            recv_sem=recv_sems.at[c, stage],
            device_id={axis: partner},
            device_id_type=MESH,
        )
        copy.start()
        pending[c] = (copy, kept)

    for c, (low, size) in enumerate(chunks):
        launch(c, 0, dense(sent_ref, low, size), dense(kept_ref, low, size), ("seq", 0))
    fill(kept_ref, [jnp.where(first, e, o) for e, o in zip(even, odd)])
    row_ref[...] = lax.dot_general(
        grad, weight_ref[...], BOTH_LAST, preferred_element_type=jnp.float32
    ).astype(jnp.bfloat16)
    for stage in range(1, stages):
        for c in range(len(chunks)):
            copy, kept = pending[c]
            copy.wait()
            current = landing[c][stage - 1]
            current[...] += kept[...]
            bit = orders[c % 2][stage]
            ahead = (slice(None),) * names[c].index(bit)
            names[c].remove(bit)
            digit = digits[bit][1]
            launch(c, stage, current.at[ahead + (1 - digit,)], current.at[ahead + (digit,)], bit)
    for c, (low, size) in enumerate(chunks):
        copy, kept = pending[c]
        copy.wait()
        total = landing[c][stages - 1][...] + kept[...]
        out_ref[low:low + size] = total / (dp_count * labels_ref.shape[0])


def shards(enc_rows, out_weight, labels, label_count, frame_count):
    utterances, frames, width = enc_rows.shape
    vocabulary = out_weight.shape[1]
    length = labels.shape[1]
    slots = length + 1
    pack = LANES // slots
    groups = utterances // pack
    seq_count = lax.axis_size("seq")
    flat_rows = enc_rows.reshape(utterances * frames, width)
    vmem = pl.BlockSpec(memory_space=pltpu.VMEM)

    rows = 2 * utterances
    steps = seq_count * frames
    dp_count = lax.axis_size("dp")
    held = halving_plan(seq_count, dp_count)[0]
    block_rows, block_columns = width // dp_count, vocabulary // seq_count
    whole_block = (2,) * len(held) + (block_rows, block_columns)
    chunks = row_chunks(block_rows)
    landed = [
        pltpu.VMEM((2,) * (len(held) - stage) + (size, block_columns), jnp.float32)
        for low, size in chunks
        for stage in range(len(held) + 1)
    ]
    smem = pl.BlockSpec(memory_space=pltpu.SMEM)
    logit_grad, row_grad, weight_grad = pl.pallas_call(
        functools.partial(fused_kernel, seq_count, dp_count),
        out_shape=(
            jax.ShapeDtypeStruct((utterances * frames, vocabulary), jnp.bfloat16),
            jax.ShapeDtypeStruct((utterances * frames, width), jnp.bfloat16),
            jax.ShapeDtypeStruct((block_rows, block_columns), jnp.float32),
        ),
        in_specs=[smem, smem] + [vmem] * 3,
        out_specs=(vmem, vmem, vmem),
        scratch_shapes=[
            pltpu.VMEM((utterances * frames, vocabulary), jnp.float32),
            pltpu.VMEM((seq_count, groups, frames, LANES), jnp.float32),
            pltpu.VMEM((rows, LANES), jnp.int32),
            pltpu.VMEM((steps, 2 * SPLIT, rows, LANES), jnp.float32),
            pltpu.VMEM((steps, 2 * SPLIT, rows, LANES), jnp.float32),
            pltpu.VMEM((SPLIT + 1, frames, rows, LANES), jnp.float32),
            pltpu.VMEM(whole_block, jnp.float32),
            pltpu.VMEM(whole_block, jnp.float32),
            pltpu.SemaphoreType.DMA((seq_count - 1,)),
            pltpu.SemaphoreType.DMA((seq_count - 1,)),
            pltpu.SemaphoreType.DMA((len(chunks), len(held) + 1)),
            pltpu.SemaphoreType.DMA((len(chunks), len(held) + 1)),
        ] + landed,
        compiler_params=pltpu.CompilerParams(
            collective_id=0, has_side_effects=True, vmem_limit_bytes=60 * 1024 * 1024
        ),
        name="fused",
    )(label_count, frame_count, flat_rows, out_weight, labels)
    return (
        logit_grad.reshape(utterances, frames, vocabulary),
        row_grad.reshape(utterances, frames, width),
        weight_grad,
    )


def solution(mesh):
    placed = (P("dp", "seq", None), P(), P("dp", None), P("dp"), P("dp"))
    return jax.shard_map(
        shards,
        mesh=mesh,
        in_specs=placed,
        out_specs=(P("dp", "seq", None), P("dp", "seq", None), P("dp", "seq")),
        check_vma=False,
    )
```

profile of v0, /device:TPU:0, one launch (start us, length us, event | category | flops | bytes accessed | tf_op | source)
XLA Modules:
  0.0 53.4 jit_solution(3007658215040116169)
XLA Ops:
  0.6 48.4 %fused.1 = (bf16[256,512]{1,0:T(8,128)(2,1)}, bf16[256,1280]{1,0:T(8,128)(2,1)}, f32[160,128]{1,0:T(8,128)}) custom-call(s32[4]{0:T(128)} %label_count_ref.1, s32[4]{0:T(128)} %frame_count_ref.1, bf16[256,1280]{1,0:T(8,128)(2,1)} %bitcast.3, bf16[1280,512]{1,0:T(8,128)(2,1)} %weight_ref.1, s32[4,63]{1,0:T(4,128)} %labels_ref.1), custom_call_target="tpu_custom_call" | custom-call | tf_op jit(solution)/shard_map/fused/pallas_call | solution.py:403
  49.0 0.0 copy-start
  49.0 1.7 %copy.11 = bf16[4,64,512]{2,1,0:T(8,128)(2,1)} copy(bf16[4,64,512]{2,1,0:T(8,128)(2,1)} %bitcast.5) | data formatting | bytes 524288
  50.8 2.0 %copy.12 = bf16[4,64,1280]{2,1,0:T(8,128)(2,1)} copy(bf16[4,64,1280]{2,1,0:T(8,128)(2,1)} %bitcast.4) | data formatting | bytes 1310720
  52.7 0.0 copy-done
  52.7 0.6 %copy.13 = f32[160,128]{1,0:T(8,128)} copy(f32[160,128]{1,0:T(8,128)S(1)} %copy-done) | data formatting | bytes 163840
Async XLA Ops:
  49.0 3.7 %copy-start = (f32[160,128]{1,0:T(8,128)S(1)}, f32[160,128]{1,0:T(8,128)}, u32[]{:S(2)}) copy-start(f32[160,128]{1,0:T(8,128)} %get-tuple-element.14) | copy-start | bytes 245764
where the time goes:
time: 53.6 us; the launch traced here: 53.4 us
  Pallas kernels  48.4 us (90%)
  local copies, waits for them, and re-layouts  4.31 us (8%)
  between operations  0.65 us (1%)
    pallas_call x1, Pallas kernels, shards(): pl.pallas_call(functools.partial(fused_kernel, seq_count, dp_count), out_...  48.4 us
    unnamed x5, local copies, waits for them, and re-layouts  4.31 us

commit v1 on v0

v1 whole, which is shorter than its diff:
```python
import functools

import jax
import jax.numpy as jnp
from jax import lax
from jax.experimental import pallas as pl
from jax.experimental.pallas import tpu as pltpu
from jax.sharding import PartitionSpec as P

negative_fill = -1e30
LOG2_E = 1.4426950408889634
LANES = 128
SUBLANES = 8
SPLIT = 2
UNROLL = 32
MESH = pl.DeviceIdType.MESH
BOTH_LAST = (((1,), (1,)), ((), ()))


def three_parts(values):
    high = values.astype(jnp.bfloat16)
    rest = values - high.astype(jnp.float32)
    middle = rest.astype(jnp.bfloat16)
    low = (rest - middle.astype(jnp.float32)).astype(jnp.bfloat16)
    return high, middle, low


def label_table(labels_ref, table_ref):
    utterances, length = labels_ref.shape
    table_ref[...] = jnp.zeros_like(table_ref)
    table_ref[0:utterances, 0:length] = labels_ref[...]
    table_ref[utterances:2 * utterances, 0:length] = labels_ref[...]
    return table_ref[...]


def take_lanes(values, index):
    return jnp.take_along_axis(values, index, axis=1)


def character_tables(labels_ref, table_ref, hot_ref):
    groups, _, vocabulary = hot_ref.shape
    utterances, length = labels_ref.shape
    slots = length + 1
    pack = utterances // groups
    width = slots // SPLIT
    table = label_table(labels_ref, table_ref)
    lane = lax.broadcasted_iota(jnp.int32, table.shape, 1)
    within = lax.rem(lane, slots)
    order = lax.rem(within, width) * SPLIT + within // width
    chars = take_lanes(table, order).astype(jnp.float32)
    row_lane = lax.broadcasted_iota(jnp.int32, (1, LANES), 1)
    columns = lax.broadcasted_iota(jnp.int32, (LANES, LANES), 1).astype(jnp.float32)
    for group in range(groups):
        first = group * pack
        line = chars[first:first + 1, :]
        for inner in range(1, pack):
            line = jnp.where(row_lane >= inner * slots, chars[first + inner:first + inner + 1, :], line)
        down = jnp.transpose(jnp.broadcast_to(line, (LANES, LANES)))
        for low in range(0, vocabulary, LANES):
            hot_ref[group, :, low:low + LANES] = jnp.where(
                down == columns + float(low), 1.0, 0.0
            ).astype(jnp.bfloat16)


def share_emissions(seq_count, enc_ref, weight_ref, labels_ref, prob_ref, gathered_ref, hot_ref,
                    table_ref, send_sems, recv_sems, before_sending, meanwhile):
    utterances, length = labels_ref.shape
    me = lax.axis_index("seq")
    frames = enc_ref.shape[0] // utterances
    groups = gathered_ref.shape[0]
    pack = utterances // groups
    slots = length + 1
    own = pl.ds(pl.multiple_of(me * frames, frames), frames)
    character_tables(labels_ref, table_ref, hot_ref)
    logits = jnp.dot(enc_ref[...], weight_ref[...], preferred_element_type=jnp.float32)
    highest = jnp.max(logits, axis=1, keepdims=True)
    shifted = logits - highest
    powers = jnp.exp(shifted)
    total = jnp.sum(powers, axis=1, keepdims=True)
    logprob = shifted - jnp.log(total)
    prob_ref[...] = powers * (1.0 / total)
    lane = lax.broadcasted_iota(jnp.int32, (frames, LANES), 1)
    for group in range(groups):
        rows = pack * frames
        mine = logprob[group * rows:(group + 1) * rows]
        picked = None
        for part in three_parts(mine):
            product = lax.dot_general(part, hot_ref[group], BOTH_LAST, preferred_element_type=jnp.float32)
            picked = product if picked is None else picked + product
        packed = picked[:frames]
        for inner in range(1, pack):
            packed = jnp.where(lane >= inner * slots, picked[inner * frames:(inner + 1) * frames], packed)
        gathered_ref[group, own, :] = packed * LOG2_E
    before_sending()
    copies = []
    for step in range(1, seq_count):
        peer = lax.rem(me + step, seq_count)
        copy = pltpu.make_async_remote_copy(
            src_ref=gathered_ref.at[:, own],
            dst_ref=gathered_ref.at[:, own],
            send_sem=send_sems.at[step - 1],
            recv_sem=recv_sems.at[step - 1],
            device_id={"seq": peer},
            device_id_type=MESH,
        )
        copy.start()
        copies.append(copy)
    meanwhile()
    for copy in copies:
        copy.wait()


def spread(count_ref, utterance):
    values = jnp.full(utterance.shape, count_ref[0], jnp.int32)
    for u in range(1, count_ref.shape[0]):
        values = jnp.where(utterance == u, count_ref[u], values)
    return values


def lattice_gradients(label_count_ref, frame_count_ref, gathered_ref, labels_ref, prob_ref, hot_ref,
                      logit_ref, table_ref, ahead_ref, back_ref, mass_ref):
    utterances, length = labels_ref.shape
    groups, steps = gathered_ref.shape[:2]
    frames = prob_ref.shape[0] // utterances
    rows = 2 * utterances
    slots = length + 1
    width = slots // SPLIT
    pack = utterances // groups
    span = LANES * SPLIT
    shape = (rows, LANES)
    row = lax.broadcasted_iota(jnp.int32, shape, 0)
    lane = lax.broadcasted_iota(jnp.int32, shape, 1)
    forward = row < utterances
    utterance = lax.rem(row, utterances)
    offset = lax.rem(utterance, pack) * slots
    label_rows = table_ref[...]
    label_count = spread(label_count_ref, utterance)
    frame_count = spread(frame_count_ref, utterance)
    first_usable = jnp.where(forward, 0, steps - frame_count)

    label_fill, jump_fill, label_start, blank_start = [], [], [], []
    for r in range(SPLIT):
        run = jnp.where(forward, r, SPLIT - 1 - r)
        j = lane * SPLIT + run
        real = j < length
        label_fill.append(jnp.where(real, 0.0, negative_fill))
        before = jnp.where(forward, j - 1, j + 1)
        here_char = take_lanes(label_rows, jnp.clip(j, 0, LANES - 1))
        before_char = take_lanes(label_rows, jnp.clip(before, 0, LANES - 1))
        can_jump = real & (before >= 0) & (before < length) & (here_char != before_char)
        jump_fill.append(jnp.where(can_jump, 0.0, negative_fill))
        label_begin = j == jnp.where(forward, 0, label_count - 1)
        label_start.append(jnp.where(label_begin, 0.0, negative_fill))
        blank = jnp.where(forward, j, lax.rem(j + 1, span))
        blank_begin = blank == jnp.where(forward, 0, label_count)
        blank_start.append(jnp.where(blank_begin, 0.0, negative_fill))
    blank_index = offset + slots - 1
    inner_of = lax.rem(utterance, pack)
    row_group = utterance // pack

    def frame_row(group, step):
        return jnp.broadcast_to(gathered_ref[group, pl.ds(step, 1), :], shape)

    def raw_emission(step):
        raw = None
        for group in range(groups):
            early = frame_row(group, step)
            late = frame_row(group, steps - 1 - step)
            both = jnp.where(forward, early, late)
            raw = both if raw is None else jnp.where(row_group == group, both, raw)
        return raw

    def label_emissions(raw):
        turned = {}
        for begin in range(0, pack * slots, width):
            turned[begin] = pltpu.roll(raw, LANES - begin, 1) if begin else raw
        found = []
        for r in range(SPLIT):
            chosen = None
            for inner in range(pack):
                ahead = turned[inner * slots + r * width]
                back = turned[inner * slots + (SPLIT - 1 - r) * width]
                both = jnp.where(forward, ahead, back)
                chosen = both if chosen is None else jnp.where(inner_of == inner, both, chosen)
            found.append(chosen + label_fill[r])
        return found

    def behind(values):
        return jnp.where(forward, pltpu.roll(values, 1, 1), pltpu.roll(values, LANES - 1, 1))

    def one_step(step, state, resets):
        labels_v, blanks_v, labels_x, blanks_x = state
        raw = raw_emission(step)
        blank_emission = take_lanes(raw, blank_index)
        label_emission = label_emissions(raw)
        ahead_row = pl.ds(pl.multiple_of(step * rows, rows), rows)
        back_row = pl.ds(pl.multiple_of((steps - 1 - step) * rows, rows), rows)
        full_labels, full_blanks = [], []
        for r in range(SPLIT):
            full_labels.append(labels_v[r] + label_emission[r])
            full_blanks.append(blanks_v[r] + blank_emission)
            ahead_ref[r, ahead_row, :] = full_labels[r]
            ahead_ref[SPLIT + r, ahead_row, :] = full_blanks[r]
            ahead_ref[2 * SPLIT + r, ahead_row, :] = labels_x[r]
            ahead_ref[3 * SPLIT + r, ahead_row, :] = blanks_x[r]
            back_ref[r, back_row, :] = labels_v[r]
            back_ref[SPLIT + r, back_row, :] = blanks_v[r]
            back_ref[2 * SPLIT + r, back_row, :] = labels_x[r]
            back_ref[3 * SPLIT + r, back_row, :] = blanks_x[r]
        if resets:
            usable = step >= first_usable
        next_labels_v, next_blanks_v, next_labels_x, next_blanks_x = [], [], [], []
        for r in range(SPLIT):
            if r == 0:
                behind_v = behind(full_labels[SPLIT - 1])
                behind_x = behind(labels_x[SPLIT - 1])
            else:
                behind_v = full_labels[r - 1]
                behind_x = labels_x[r - 1]
            jump_v = behind_v + jump_fill[r]
            pivot = jnp.maximum(jnp.maximum(full_blanks[r], full_labels[r]), jump_v)
            fresh_x = (
                jnp.exp2(full_labels[r] - pivot) * labels_x[r]
                + jnp.exp2(full_blanks[r] - pivot) * blanks_x[r]
                + jnp.exp2(jump_v - pivot) * behind_x
            )
            if resets:
                pivot = jnp.where(usable, pivot, label_start[r])
                fresh_x = jnp.where(usable, fresh_x, 1.0)
            next_labels_v.append(pivot)
            next_labels_x.append(fresh_x)
            pivot = jnp.maximum(full_blanks[r], behind_v)
            fresh_x = (
                jnp.exp2(full_blanks[r] - pivot) * blanks_x[r]
                + jnp.exp2(behind_v - pivot) * behind_x
            )
            if resets:
                pivot = jnp.where(usable, pivot, blank_start[r])
                fresh_x = jnp.where(usable, fresh_x, 1.0)
            next_blanks_v.append(pivot)
            next_blanks_x.append(fresh_x)
        return (tuple(next_labels_v), tuple(next_blanks_v), tuple(next_labels_x), tuple(next_blanks_x))

    ones = (jnp.ones(shape, jnp.float32),) * SPLIT

    def run_block(resets, block, state):
        labels_v, blanks_v = state
        full = (labels_v, blanks_v, ones, ones)
        for inner in range(UNROLL):
            full = one_step(block * UNROLL + inner, full, resets)
        labels_v, blanks_v, labels_x, blanks_x = full
        labels_v = tuple(v + jnp.log2(x) for v, x in zip(labels_v, labels_x))
        blanks_v = tuple(v + jnp.log2(x) for v, x in zip(blanks_v, blanks_x))
        return labels_v, blanks_v

    blocks = steps // UNROLL
    resetting = (steps // 2) // UNROLL
    state = (tuple(label_start), tuple(blank_start))
    state = lax.fori_loop(0, resetting, functools.partial(run_block, True), state)
    lax.fori_loop(resetting, blocks, functools.partial(run_block, False), state)

    start = lax.axis_index("seq") * frames
    inner_frame = row // utterances

    def posterior_block(block, carry):
        for pair in range(0, SUBLANES, 2):
            low = block * SUBLANES + pair
            first = pl.multiple_of((start + low) * rows, rows)

            def ahead(index):
                return jnp.where(
                    forward, ahead_ref[index, pl.ds(first, rows), :],
                    ahead_ref[index, pl.ds(first + utterances, rows), :],
                )

            def back(index):
                return jnp.where(
                    forward, back_ref[index, pl.ds(first + utterances, rows), :],
                    back_ref[index, pl.ds(first + rows, rows), :],
                )

            def term(ahead_index, back_index, turn):
                level, factor = back(back_index), back(2 * SPLIT + back_index)
                if turn:
                    level, factor = pltpu.roll(level, 1, 1), pltpu.roll(factor, 1, 1)
                factor = factor * ahead(2 * SPLIT + ahead_index)
                return (ahead(ahead_index) + level) + jnp.log2(factor)

            terms = [term(r, SPLIT - 1 - r, False) for r in range(SPLIT)]
            terms += [term(SPLIT + r, SPLIT + (SPLIT - r) % SPLIT, r == 0) for r in range(SPLIT)]
            highest = jnp.max(functools.reduce(jnp.maximum, terms), axis=1, keepdims=True)
            powers = [jnp.exp2(value - highest) for value in terms]
            blank_mass = jnp.sum(functools.reduce(jnp.add, powers[SPLIT:]), axis=1, keepdims=True)
            total = blank_mass + jnp.sum(functools.reduce(jnp.add, powers[:SPLIT]), axis=1, keepdims=True)
            usable = start + low + inner_frame < frame_count
            scale = jnp.where(usable, 1.0 / total, 0.0)
            mass = jnp.where(lane == offset + slots - 1, blank_mass, 0.0)
            for inner in range(pack):
                spread_out = None
                for r in range(SPLIT):
                    shift = inner * slots + r * width
                    moved = pltpu.roll(powers[r], shift, 1) if shift else powers[r]
                    spread_out = moved if spread_out is None else spread_out + moved
                mass += spread_out if pack == 1 else jnp.where(inner_of == inner, spread_out, 0.0)
            mass_ref[pl.ds(pl.multiple_of(low * utterances, rows), rows), :] = mass * scale
        return carry

    lax.fori_loop(0, frames // SUBLANES, posterior_block, 0)

    times = start + lax.broadcasted_iota(jnp.int32, (frames, 1), 0)
    for u in range(utterances):
        own = slice(u * frames, (u + 1) * frames)
        hot = hot_ref[u // pack]
        mass = None
        for part in three_parts(mass_ref[pl.ds(u, frames, stride=utterances), :])[:2]:
            product = jnp.dot(part, hot, preferred_element_type=jnp.float32)
            mass = product if mass is None else mass + product
        kept = jnp.where(times < frame_count_ref[u], prob_ref[own, :] - mass, 0.0)
        logit_ref[own, :] = kept.astype(jnp.bfloat16)
def binary_digits(axis, count):
    index = lax.axis_index(axis)
    digits = []
    step = 1
    while step < count:
        digit = lax.rem(index // step, 2)
        digits.append((axis, digit, index + step * (1 - 2 * digit)))
        step *= 2
    return digits


def halving_plan(seq_count, dp_count):
    seq_bits = [("seq", i) for i in range(seq_count.bit_length() - 1)]
    dp_bits = [("dp", i) for i in range(dp_count.bit_length() - 1)]
    first, others = seq_bits[:1], seq_bits[1:]
    along = first + others + dp_bits
    across = first + dp_bits[:1] + others + dp_bits[1:]
    held = others[::-1] + dp_bits[::-1]
    return held, (along, across)


def row_chunks(rows):
    quarter = -(-rows // 10 // 8) * 8
    return [(low, min(quarter, rows - low)) for low in range(0, rows, quarter)]


def fused_kernel(seq_count, dp_count, label_count_ref, frame_count_ref, enc_ref, weight_ref,
                 labels_ref, logit_ref, row_ref, out_ref, prob_ref, gathered_ref, hot_ref, table_ref,
                 turned_ref, ahead_ref, back_ref, mass_ref, sent_ref, kept_ref, share_send, share_recv,
                 send_sems, recv_sems, *landed):
    me = lax.axis_index("seq")
    digits = {
        (axis, i): entry
        for axis, count in (("seq", seq_count), ("dp", dp_count))
        for i, entry in enumerate(binary_digits(axis, count))
    }
    greeted = [("seq", lax.rem(me + step, seq_count)) for step in range(1, seq_count)]
    greeted += [(axis, partner) for axis, _, partner in digits.values() if axis == "dp"]
    barrier = pltpu.get_barrier_semaphore()
    for axis, partner in greeted:
        pl.semaphore_signal(barrier, inc=1, device_id={axis: partner}, device_id_type=MESH)

    def before_sending():
        pl.semaphore_wait(barrier, len(greeted))

    def meanwhile():
        turned_ref[...] = jnp.transpose(enc_ref[...])

    share_emissions(seq_count, enc_ref, weight_ref, labels_ref, prob_ref, gathered_ref, hot_ref,
                    table_ref, share_send, share_recv, before_sending, meanwhile)
    lattice_gradients(label_count_ref, frame_count_ref, gathered_ref, labels_ref, prob_ref, hot_ref,
                      logit_ref, table_ref, ahead_ref, back_ref, mass_ref)

    grad = logit_ref[...]
    columns = sent_ref.shape[-1]
    core = digits[("seq", 0)][1]
    even = [grad[:, s * columns:(s + 1) * columns] for s in range(0, seq_count, 2)]
    odd = [grad[:, s * columns:(s + 1) * columns] for s in range(1, seq_count, 2)]

    def fill(target_ref, halves):
        product = jnp.dot(
            turned_ref[...], jnp.concatenate(halves, axis=1), preferred_element_type=jnp.float32
        )
        high = (seq_count // 2).bit_length() - 1
        for h in range(seq_count // 2):
            place = tuple((h >> (high - 1 - i)) & 1 for i in range(high))
            piece = product[:, h * columns:(h + 1) * columns]
            target_ref[place] = piece.reshape(target_ref.shape[high:])

    first = core == 0
    fill(sent_ref, [jnp.where(first, o, e) for e, o in zip(even, odd)])

    held, orders = halving_plan(seq_count, dp_count)
    rows = out_ref.shape[0]
    chunks = row_chunks(rows)
    stages = len(held) + 1
    landing = [landed[c * stages:(c + 1) * stages] for c in range(len(chunks))]
    names = [list(held) for _ in chunks]
    pending = [None] * len(chunks)

    def dense(ref, low, size):
        return ref.at[(slice(None),) * len(held) + (pl.ds(low, size),)]

    def launch(c, stage, source, kept, bit):
        axis, _, partner = digits[bit]
        copy = pltpu.make_async_remote_copy(
            src_ref=source,
            dst_ref=landing[c][stage],
            send_sem=send_sems.at[c, stage],
            recv_sem=recv_sems.at[c, stage],
            device_id={axis: partner},
            device_id_type=MESH,
        )
        copy.start()
        pending[c] = (copy, kept)

    for c, (low, size) in enumerate(chunks):
        launch(c, 0, dense(sent_ref, low, size), dense(kept_ref, low, size), ("seq", 0))
    fill(kept_ref, [jnp.where(first, e, o) for e, o in zip(even, odd)])
    row_ref[...] = lax.dot_general(
        grad, weight_ref[...], BOTH_LAST, preferred_element_type=jnp.float32
    ).astype(jnp.bfloat16)
    for stage in range(1, stages):
        for c in range(len(chunks)):
            copy, kept = pending[c]
            copy.wait()
            current = landing[c][stage - 1]
            current[...] += kept[...]
            bit = orders[c % 2][stage]
            ahead = (slice(None),) * names[c].index(bit)
            names[c].remove(bit)
            digit = digits[bit][1]
            launch(c, stage, current.at[ahead + (1 - digit,)], current.at[ahead + (digit,)], bit)
    for c, (low, size) in enumerate(chunks):
        copy, kept = pending[c]
        copy.wait()
        total = landing[c][stages - 1][...] + kept[...]
        out_ref[low:low + size] = total / (dp_count * labels_ref.shape[0])


def shards(enc_rows, out_weight, labels, label_count, frame_count):
    utterances, frames, width = enc_rows.shape
    vocabulary = out_weight.shape[1]
    length = labels.shape[1]
    slots = length + 1
    pack = LANES // slots
    groups = utterances // pack
    seq_count = lax.axis_size("seq")
    flat_rows = enc_rows.reshape(utterances * frames, width)
    vmem = pl.BlockSpec(memory_space=pltpu.VMEM)

    rows = 2 * utterances
    steps = seq_count * frames
    dp_count = lax.axis_size("dp")
    held = halving_plan(seq_count, dp_count)[0]
    block_rows, block_columns = width // dp_count, vocabulary // seq_count
    whole_block = (2,) * len(held) + (block_rows, block_columns)
    chunks = row_chunks(block_rows)
    landed = [
        pltpu.VMEM((2,) * (len(held) - stage) + (size, block_columns), jnp.float32)
        for low, size in chunks
        for stage in range(len(held) + 1)
    ]
    smem = pl.BlockSpec(memory_space=pltpu.SMEM)
    logit_grad, row_grad, weight_grad = pl.pallas_call(
        functools.partial(fused_kernel, seq_count, dp_count),
        out_shape=(
            jax.ShapeDtypeStruct((utterances * frames, vocabulary), jnp.bfloat16),
            jax.ShapeDtypeStruct((utterances * frames, width), jnp.bfloat16),
            jax.ShapeDtypeStruct((block_rows, block_columns), jnp.float32),
        ),
        in_specs=[smem, smem] + [vmem] * 3,
        out_specs=(vmem, vmem, vmem),
        scratch_shapes=[
            pltpu.VMEM((utterances * frames, vocabulary), jnp.float32),
            pltpu.VMEM((groups, steps, LANES), jnp.float32),
            pltpu.VMEM((groups, LANES, vocabulary), jnp.bfloat16),
            pltpu.VMEM((rows, LANES), jnp.int32),
            pltpu.VMEM((width, utterances * frames), jnp.bfloat16),
            pltpu.VMEM((4 * SPLIT, steps * rows, LANES), jnp.float32),
            pltpu.VMEM((4 * SPLIT, steps * rows, LANES), jnp.float32),
            pltpu.VMEM((utterances * frames, LANES), jnp.float32),
            pltpu.VMEM(whole_block, jnp.float32),
            pltpu.VMEM(whole_block, jnp.float32),
            pltpu.SemaphoreType.DMA((seq_count - 1,)),
            pltpu.SemaphoreType.DMA((seq_count - 1,)),
            pltpu.SemaphoreType.DMA((len(chunks), len(held) + 1)),
            pltpu.SemaphoreType.DMA((len(chunks), len(held) + 1)),
        ] + landed,
        compiler_params=pltpu.CompilerParams(
            collective_id=0, has_side_effects=True, vmem_limit_bytes=60 * 1024 * 1024
        ),
        name="fused",
    )(label_count, frame_count, flat_rows, out_weight, labels)
    return (
        logit_grad.reshape(utterances, frames, vocabulary),
        row_grad.reshape(utterances, frames, width),
        weight_grad,
    )


def solution(mesh):
    placed = (P("dp", "seq", None), P(), P("dp", None), P("dp"), P("dp"))
    return jax.shard_map(
        shards,
        mesh=mesh,
        in_specs=placed,
        out_specs=(P("dp", "seq", None), P("dp", "seq", None), P("dp", "seq")),
        check_vma=False,
    )
```

time: 53.6 us -> 52.2 us (0.974)
  Pallas kernels: 48.4 us -> 47.1 us
    pallas_call x1, Pallas kernels: 48.4 us -> 47.1 us  [shards(): pl.pallas_call(functools.partial(fused_kernel, seq_count, dp_count), out_...]
where the time goes in v1:
time: 52.2 us; the launch traced here: 52 us
  Pallas kernels  47.1 us (90%)
  local copies, waits for them, and re-layouts  4.31 us (8%)
  between operations  0.65 us (1%)
    pallas_call x1, Pallas kernels, shards(): pl.pallas_call(functools.partial(fused_kernel, seq_count, dp_count), out_...  47.1 us
    unnamed x5, local copies, waits for them, and re-layouts  4.31 us

profile of v1, /device:TPU:0, one launch (start us, length us, event | category | flops | bytes accessed | tf_op | source)
XLA Modules:
  0.0 52.0 jit_solution(1073145379284046424)
XLA Ops:
  0.6 47.1 %fused.1 = (bf16[256,512]{1,0:T(8,128)(2,1)}, bf16[256,1280]{1,0:T(8,128)(2,1)}, f32[160,128]{1,0:T(8,128)}) custom-call(s32[4]{0:T(128)} %label_count_ref.1, s32[4]{0:T(128)} %frame_count_ref.1, bf16[256,1280]{1,0:T(8,128)(2,1)} %bitcast.3, bf16[1280,512]{1,0:T(8,128)(2,1)} %weight_ref.1, s32[4,63]{1,0:T(4,128)} %labels_ref.1), custom_call_target="tpu_custom_call" | custom-call | tf_op jit(solution)/shard_map/fused/pallas_call | solution.py:464
  47.7 0.0 copy-start
  47.7 1.7 %copy.11 = bf16[4,64,512]{2,1,0:T(8,128)(2,1)} copy(bf16[4,64,512]{2,1,0:T(8,128)(2,1)} %bitcast.5) | data formatting | bytes 524288
  49.4 2.0 %copy.12 = bf16[4,64,1280]{2,1,0:T(8,128)(2,1)} copy(bf16[4,64,1280]{2,1,0:T(8,128)(2,1)} %bitcast.4) | data formatting | bytes 1310720
  51.4 0.0 copy-done
  51.4 0.6 %copy.13 = f32[160,128]{1,0:T(8,128)} copy(f32[160,128]{1,0:T(8,128)S(1)} %copy-done) | data formatting | bytes 163840
Async XLA Ops:
  47.7 3.7 %copy-start = (f32[160,128]{1,0:T(8,128)S(1)}, f32[160,128]{1,0:T(8,128)}, u32[]{:S(2)}) copy-start(f32[160,128]{1,0:T(8,128)} %get-tuple-element.14) | copy-start | bytes 245764

commit v2 on v1

--- a/solution.py
+++ b/solution.py
@@ -11,7 +11,7 @@
 LOG2_E = 1.4426950408889634
 LANES = 128
 SUBLANES = 8
-SPLIT = 2
+SPLIT = 4
 UNROLL = 32
 MESH = pl.DeviceIdType.MESH
 BOTH_LAST = (((1,), (1,)), ((), ()))
@@ -123,6 +123,7 @@
     groups, steps = gathered_ref.shape[:2]
     frames = prob_ref.shape[0] // utterances
     rows = 2 * utterances
+    stored = 4 * SPLIT * rows
     slots = length + 1
     width = slots // SPLIT
     pack = utterances // groups
@@ -188,25 +189,25 @@
     def behind(values):
         return jnp.where(forward, pltpu.roll(values, 1, 1), pltpu.roll(values, LANES - 1, 1))
 
-    def one_step(step, state, resets):
+    def one_step(step, ahead_slot, back_slot, state, resets):
         labels_v, blanks_v, labels_x, blanks_x = state
         raw = raw_emission(step)
         blank_emission = take_lanes(raw, blank_index)
         label_emission = label_emissions(raw)
-        ahead_row = pl.ds(pl.multiple_of(step * rows, rows), rows)
-        back_row = pl.ds(pl.multiple_of((steps - 1 - step) * rows, rows), rows)
+        ahead_row = pl.multiple_of(ahead_slot * stored, rows)
+        back_row = pl.multiple_of(back_slot * stored, rows)
         full_labels, full_blanks = [], []
         for r in range(SPLIT):
             full_labels.append(labels_v[r] + label_emission[r])
             full_blanks.append(blanks_v[r] + blank_emission)
-            ahead_ref[r, ahead_row, :] = full_labels[r]
-            ahead_ref[SPLIT + r, ahead_row, :] = full_blanks[r]
-            ahead_ref[2 * SPLIT + r, ahead_row, :] = labels_x[r]
-            ahead_ref[3 * SPLIT + r, ahead_row, :] = blanks_x[r]
-            back_ref[r, back_row, :] = labels_v[r]
-            back_ref[SPLIT + r, back_row, :] = blanks_v[r]
-            back_ref[2 * SPLIT + r, back_row, :] = labels_x[r]
-            back_ref[3 * SPLIT + r, back_row, :] = blanks_x[r]
+            ahead_ref[pl.ds(ahead_row + (r) * rows, rows), :] = full_labels[r]
+            ahead_ref[pl.ds(ahead_row + (SPLIT + r) * rows, rows), :] = full_blanks[r]
+            ahead_ref[pl.ds(ahead_row + (2 * SPLIT + r) * rows, rows), :] = labels_x[r]
+            ahead_ref[pl.ds(ahead_row + (3 * SPLIT + r) * rows, rows), :] = blanks_x[r]
+            back_ref[pl.ds(back_row + (r) * rows, rows), :] = labels_v[r]
+            back_ref[pl.ds(back_row + (SPLIT + r) * rows, rows), :] = blanks_v[r]
+            back_ref[pl.ds(back_row + (2 * SPLIT + r) * rows, rows), :] = labels_x[r]
+            back_ref[pl.ds(back_row + (3 * SPLIT + r) * rows, rows), :] = blanks_x[r]
         if resets:
             usable = step >= first_usable
         next_labels_v, next_blanks_v, next_labels_x, next_blanks_x = [], [], [], []
@@ -243,11 +244,22 @@
 
     ones = (jnp.ones(shape, jnp.float32),) * SPLIT
 
+    me = lax.axis_index("seq")
+    seq_count = steps // frames
+
+    def history_slot(frame):
+        away = lax.rem(frame // frames - me + seq_count, seq_count)
+        return (away + seq_count - 1) // seq_count * frames + lax.rem(frame, frames)
+
     def run_block(resets, block, state):
         labels_v, blanks_v = state
         full = (labels_v, blanks_v, ones, ones)
+        ahead_slot = history_slot(block * UNROLL)
+        back_slot = history_slot(steps - (block + 1) * UNROLL)
         for inner in range(UNROLL):
-            full = one_step(block * UNROLL + inner, full, resets)
+            full = one_step(
+                block * UNROLL + inner, ahead_slot + inner, back_slot + UNROLL - 1 - inner, full, resets
+            )
         labels_v, blanks_v, labels_x, blanks_x = full
         labels_v = tuple(v + jnp.log2(x) for v, x in zip(labels_v, labels_x))
         blanks_v = tuple(v + jnp.log2(x) for v, x in zip(blanks_v, blanks_x))
@@ -259,24 +271,24 @@
     state = lax.fori_loop(0, resetting, functools.partial(run_block, True), state)
     lax.fori_loop(resetting, blocks, functools.partial(run_block, False), state)
 
-    start = lax.axis_index("seq") * frames
+    start = me * frames
     inner_frame = row // utterances
 
     def posterior_block(block, carry):
         for pair in range(0, SUBLANES, 2):
             low = block * SUBLANES + pair
-            first = pl.multiple_of((start + low) * rows, rows)
+            first = pl.multiple_of(low * stored, rows)
 
             def ahead(index):
                 return jnp.where(
-                    forward, ahead_ref[index, pl.ds(first, rows), :],
-                    ahead_ref[index, pl.ds(first + utterances, rows), :],
+                    forward, ahead_ref[pl.ds(first + index * rows, rows), :],
+                    ahead_ref[pl.ds(first + stored + index * rows - utterances, rows), :],
                 )
 
             def back(index):
                 return jnp.where(
-                    forward, back_ref[index, pl.ds(first + utterances, rows), :],
-                    back_ref[index, pl.ds(first + rows, rows), :],
+                    forward, back_ref[pl.ds(first + index * rows + utterances, rows), :],
+                    back_ref[pl.ds(first + stored + index * rows, rows), :],
                 )
 
             def term(ahead_index, back_index, turn):
@@ -437,6 +449,18 @@
         out_ref[low:low + size] = total / (dp_count * labels_ref.shape[0])
 
 
+def write_results(*refs):
+    sems = refs[-1]
+    count = (len(refs) - 1) // 2
+    copies = [
+        pltpu.make_async_copy(refs[i], refs[count + i], sems.at[i]) for i in range(count)
+    ]
+    for copy in copies:
+        copy.start()
+    for copy in copies:
+        copy.wait()
+
+
 def shards(enc_rows, out_weight, labels, label_count, frame_count):
     utterances, frames, width = enc_rows.shape
     vocabulary = out_weight.shape[1]
@@ -464,9 +488,9 @@
     logit_grad, row_grad, weight_grad = pl.pallas_call(
         functools.partial(fused_kernel, seq_count, dp_count),
         out_shape=(
-            jax.ShapeDtypeStruct((utterances * frames, vocabulary), jnp.bfloat16),
-            jax.ShapeDtypeStruct((utterances * frames, width), jnp.bfloat16),
-            jax.ShapeDtypeStruct((block_rows, block_columns), jnp.float32),
+            pltpu.VMEM((utterances * frames, vocabulary), jnp.bfloat16),
+            pltpu.VMEM((utterances * frames, width), jnp.bfloat16),
+            pltpu.VMEM((block_rows, block_columns), jnp.float32),
         ),
         in_specs=[smem, smem] + [vmem] * 3,
         out_specs=(vmem, vmem, vmem),
@@ -476,8 +500,8 @@
             pltpu.VMEM((groups, LANES, vocabulary), jnp.bfloat16),
             pltpu.VMEM((rows, LANES), jnp.int32),
             pltpu.VMEM((width, utterances * frames), jnp.bfloat16),
-            pltpu.VMEM((4 * SPLIT, steps * rows, LANES), jnp.float32),
-            pltpu.VMEM((4 * SPLIT, steps * rows, LANES), jnp.float32),
+            pltpu.VMEM((2 * frames * 4 * SPLIT * rows, LANES), jnp.float32),
+            pltpu.VMEM((2 * frames * 4 * SPLIT * rows, LANES), jnp.float32),
             pltpu.VMEM((utterances * frames, LANES), jnp.float32),
             pltpu.VMEM(whole_block, jnp.float32),
             pltpu.VMEM(whole_block, jnp.float32),
@@ -491,6 +515,19 @@
         ),
         name="fused",
     )(label_count, frame_count, flat_rows, out_weight, labels)
+    logit_grad, row_grad, weight_grad = pl.pallas_call(
+        write_results,
+        out_shape=(
+            jax.ShapeDtypeStruct((utterances * frames, vocabulary), jnp.bfloat16),
+            jax.ShapeDtypeStruct((utterances * frames, width), jnp.bfloat16),
+            jax.ShapeDtypeStruct((block_rows, block_columns), jnp.float32),
+        ),
+        in_specs=[vmem] * 3,
+        out_specs=(pl.BlockSpec(memory_space=pl.ANY),) * 3,
+        scratch_shapes=[pltpu.SemaphoreType.DMA((3,))],
+        compiler_params=pltpu.CompilerParams(vmem_limit_bytes=4 * 1024 * 1024),
+        name="write_results",
+    )(logit_grad, row_grad, weight_grad)
     return (
         logit_grad.reshape(utterances, frames, vocabulary),
         row_grad.reshape(utterances, frames, width),

time: 52.2 us -> 44.2 us (0.85)
  local copies, waits for them, and re-layouts: 4.31 us -> 0 us
  Pallas kernels: 47.1 us -> 43.5 us
    pallas_call x1, Pallas kernels: 47.1 us -> 42.5 us  [shards(): pl.pallas_call(functools.partial(fused_kernel, seq_count, dp_count), out_...]
    unnamed x5 -> x0, local copies, waits for them, and re-layouts: 4.31 us -> none
    pallas_call x0 -> x1, Pallas kernels: none -> 0.97 us  [shards(): pl.pallas_call(write_results, out_shape=(jax.ShapeDtypeStruct((utterances...]
where the time goes in v2:
time: 44.2 us; the launch traced here: 44.1 us
  Pallas kernels  43.5 us (98%)
  between operations  0.64 us (1%)
    pallas_call x1, Pallas kernels, shards(): pl.pallas_call(functools.partial(fused_kernel, seq_count, dp_count), out_...  42.5 us
    pallas_call x1, Pallas kernels, shards(): pl.pallas_call(write_results, out_shape=(jax.ShapeDtypeStruct((utterances...  0.97 us

profile of v2, /device:TPU:0, one launch (start us, length us, event | category | flops | bytes accessed | tf_op | source)
XLA Modules:
  0.0 44.1 jit_solution(15871913119039406176)
XLA Ops:
  0.6 42.5 %fused.1 = (bf16[256,512]{1,0:T(8,128)(2,1)S(1)}, bf16[256,1280]{1,0:T(8,128)(2,1)S(1)}, f32[160,128]{1,0:T(8,128)S(1)}) custom-call(s32[4]{0:T(128)} %label_count_ref.1, s32[4]{0:T(128)} %frame_count_ref.1, bf16[256,1280]{1,0:T(8,128)(2,1)} %bitcast.3, bf16[1280,512]{1,0:T(8,128)(2,1)} %weight_ref.1, s32[4,63]{1,0:T(4,128)} %labels_ref.1), custom_call_target="tpu_custom_call" | custom-call | tf_op jit(solution)/shard_map/fused/pallas_call | solution.py:488
  43.1 1.0 %write_results.1 = (bf16[256,512]{1,0:T(8,128)(2,1)}, bf16[256,1280]{1,0:T(8,128)(2,1)}, f32[160,128]{1,0:T(8,128)}) custom-call(bf16[256,512]{1,0:T(8,128)(2,1)S(1)} %get-tuple-element.9.refs_0_, bf16[256,1280]{1,0:T(8,128)(2,1)S(1)} %get-tuple-element.10.refs_1_, f32[160,128]{1,0:T(8,128)S(1)} %get-tuple-element.11.refs_2_), custom_call_target="tpu_custom_call" | custom-call | tf_op jit(solution)/shard_map/write_results/pallas_call | solution.py:518

commit v3 on v2

--- a/solution.py
+++ b/solution.py
@@ -1,4 +1,5 @@
 import functools
+import itertools
 
 import jax
 import jax.numpy as jnp
@@ -340,14 +341,69 @@
     return digits
 
 
-def halving_plan(seq_count, dp_count):
-    seq_bits = [("seq", i) for i in range(seq_count.bit_length() - 1)]
+def link_bits(seq_count, dp_count):
+    seq_bits = [("seq", i) for i in range(1, seq_count.bit_length() - 1)]
     dp_bits = [("dp", i) for i in range(dp_count.bit_length() - 1)]
-    first, others = seq_bits[:1], seq_bits[1:]
-    along = first + others + dp_bits
-    across = first + dp_bits[:1] + others + dp_bits[1:]
-    held = others[::-1] + dp_bits[::-1]
-    return held, (along, across)
+    return seq_bits, dp_bits
+
+
+def play(orders, sizes, cost):
+    free, arrivals, taken = {}, {}, []
+    clock = 0.3
+    first_left = len(orders)
+
+    def launch(chunk, stage, begin):
+        line, rate, latency = cost(orders[chunk][stage])
+        end = max(begin, free.get(line, 0.0)) + sizes[chunk] / 2 ** (stage + 1) / rate
+        free[line] = end
+        arrivals[chunk] = (end + latency, chunk, stage)
+
+    for chunk in range(len(orders)):
+        launch(chunk, 0, 0.0)
+    while arrivals:
+        arrived, chunk, stage = min(arrivals.values())
+        del arrivals[chunk]
+        clock = max(clock, arrived) + 0.01 + sizes[chunk] / 2 ** (stage + 1) / 4e6
+        taken.append((chunk, stage))
+        if stage + 1 < len(orders[chunk]):
+            launch(chunk, stage + 1, clock)
+        if stage == 0:
+            first_left -= 1
+            if first_left == 0:
+                clock += 0.45
+    return clock, taken
+
+
+def transfer_plan(seq_count, dp_count, sizes):
+    seq_bits, dp_bits = link_bits(seq_count, dp_count)
+    bits = seq_bits + dp_bits
+    core = ("seq", 0)
+
+    def cost(bit):
+        axis, i = bit
+        if bit == core:
+            return "core", 0.4e6, 0.9
+        far = 2 ** (i - 1) if i else 1
+        line = "seq" if axis == "seq" else ("dp first" if i == 0 else "dp rest")
+        return line, 0.05e6 / far, 1.0 + 0.7 * far
+
+    if len(bits) <= 4:
+        choices = [(core,) + order for order in itertools.permutations(bits)]
+    else:
+        choices = [(core,) + tuple(bits[k:] + bits[:k]) for k in range(len(bits))]
+    orders = [choices[c % len(choices)] for c in range(len(sizes))]
+    best = play(orders, sizes, cost)[0]
+    for _ in range(4):
+        before = best
+        for chunk in range(len(sizes)):
+            for choice in choices:
+                trial = orders[:chunk] + [choice] + orders[chunk + 1:]
+                length = play(trial, sizes, cost)[0]
+                if length < best:
+                    best, orders = length, trial
+        if best == before:
+            break
+    return orders, play(orders, sizes, cost)[1]
 
 
 def row_chunks(rows):
@@ -401,10 +457,14 @@
     first = core == 0
     fill(sent_ref, [jnp.where(first, o, e) for e, o in zip(even, odd)])
 
-    held, orders = halving_plan(seq_count, dp_count)
+    seq_bits, dp_bits = link_bits(seq_count, dp_count)
+    held = seq_bits[::-1] + dp_bits[::-1]
     rows = out_ref.shape[0]
     chunks = row_chunks(rows)
     stages = len(held) + 1
+    orders, taken = transfer_plan(
+        seq_count, dp_count, [size * columns * 2 ** stages * 4 for _, size in chunks]
+    )
     landing = [landed[c * stages:(c + 1) * stages] for c in range(len(chunks))]
     names = [list(held) for _ in chunks]
     pending = [None] * len(chunks)
@@ -417,7 +477,7 @@
         copy = pltpu.make_async_remote_copy(
             src_ref=source,
             dst_ref=landing[c][stage],
-            send_sem=send_sems.at[c, stage],
+            send_sem=send_sems.at[c],
             recv_sem=recv_sems.at[c, stage],
             device_id={axis: partner},
             device_id_type=MESH,
@@ -428,25 +488,25 @@
     for c, (low, size) in enumerate(chunks):
         launch(c, 0, dense(sent_ref, low, size), dense(kept_ref, low, size), ("seq", 0))
     fill(kept_ref, [jnp.where(first, e, o) for e, o in zip(even, odd)])
-    row_ref[...] = lax.dot_general(
-        grad, weight_ref[...], BOTH_LAST, preferred_element_type=jnp.float32
-    ).astype(jnp.bfloat16)
-    for stage in range(1, stages):
-        for c in range(len(chunks)):
-            copy, kept = pending[c]
-            copy.wait()
-            current = landing[c][stage - 1]
+    last_first = max(i for i, (_, stage) in enumerate(taken) if stage == 0)
+    for i, (c, stage) in enumerate(taken):
+        copy, kept = pending[c]
+        copy.wait()
+        current = landing[c][stage]
+        if stage + 1 < stages:
             current[...] += kept[...]
-            bit = orders[c % 2][stage]
+            bit = orders[c][stage + 1]
             ahead = (slice(None),) * names[c].index(bit)
             names[c].remove(bit)
             digit = digits[bit][1]
-            launch(c, stage, current.at[ahead + (1 - digit,)], current.at[ahead + (digit,)], bit)
-    for c, (low, size) in enumerate(chunks):
-        copy, kept = pending[c]
-        copy.wait()
-        total = landing[c][stages - 1][...] + kept[...]
-        out_ref[low:low + size] = total / (dp_count * labels_ref.shape[0])
+            launch(c, stage + 1, current.at[ahead + (1 - digit,)], current.at[ahead + (digit,)], bit)
+        else:
+            low, size = chunks[c]
+            out_ref[low:low + size] = (current[...] + kept[...]) / (dp_count * labels_ref.shape[0])
+        if i == last_first:
+            row_ref[...] = lax.dot_general(
+                grad, weight_ref[...], BOTH_LAST, preferred_element_type=jnp.float32
+            ).astype(jnp.bfloat16)
 
 
 def write_results(*refs):
@@ -475,7 +535,7 @@
     rows = 2 * utterances
     steps = seq_count * frames
     dp_count = lax.axis_size("dp")
-    held = halving_plan(seq_count, dp_count)[0]
+    held = sum(link_bits(seq_count, dp_count), [])
     block_rows, block_columns = width // dp_count, vocabulary // seq_count
     whole_block = (2,) * len(held) + (block_rows, block_columns)
     chunks = row_chunks(block_rows)
@@ -507,7 +567,7 @@
             pltpu.VMEM(whole_block, jnp.float32),
             pltpu.SemaphoreType.DMA((seq_count - 1,)),
             pltpu.SemaphoreType.DMA((seq_count - 1,)),
-            pltpu.SemaphoreType.DMA((len(chunks), len(held) + 1)),
+            pltpu.SemaphoreType.DMA((len(chunks),)),
             pltpu.SemaphoreType.DMA((len(chunks), len(held) + 1)),
         ] + landed,
         compiler_params=pltpu.CompilerParams(

time: 44.2 us -> 41.7 us (0.943)
  Pallas kernels: 43.5 us -> 40.9 us
    pallas_call x1, Pallas kernels: 42.5 us -> 39.9 us  [shards(): pl.pallas_call(functools.partial(fused_kernel, seq_count, dp_count), out_...]
where the time goes in v3:
time: 41.7 us; the launch traced here: 41.5 us
  Pallas kernels  40.9 us (98%)
  between operations  0.64 us (2%)
    pallas_call x1, Pallas kernels, shards(): pl.pallas_call(functools.partial(fused_kernel, seq_count, dp_count), out_...  39.9 us
    pallas_call x1, Pallas kernels, shards(): pl.pallas_call(write_results, out_shape=(jax.ShapeDtypeStruct((utterances...  0.97 us

profile of v3, /device:TPU:0, one launch (start us, length us, event | category | flops | bytes accessed | tf_op | source)
XLA Modules:
  0.0 41.5 jit_solution(8030048808822790849)
XLA Ops:
  0.6 39.9 %fused.1 = (bf16[256,512]{1,0:T(8,128)(2,1)S(1)}, bf16[256,1280]{1,0:T(8,128)(2,1)S(1)}, f32[160,128]{1,0:T(8,128)S(1)}) custom-call(s32[4]{0:T(128)} %label_count_ref.1, s32[4]{0:T(128)} %frame_count_ref.1, bf16[256,1280]{1,0:T(8,128)(2,1)} %bitcast.3, bf16[1280,512]{1,0:T(8,128)(2,1)} %weight_ref.1, s32[4,63]{1,0:T(4,128)} %labels_ref.1), custom_call_target="tpu_custom_call" | custom-call | tf_op jit(solution)/shard_map/fused/pallas_call | solution.py:548
  40.6 1.0 %write_results.1 = (bf16[256,512]{1,0:T(8,128)(2,1)}, bf16[256,1280]{1,0:T(8,128)(2,1)}, f32[160,128]{1,0:T(8,128)}) custom-call(bf16[256,512]{1,0:T(8,128)(2,1)S(1)} %get-tuple-element.9.refs_0_, bf16[256,1280]{1,0:T(8,128)(2,1)S(1)} %get-tuple-element.10.refs_1_, f32[160,128]{1,0:T(8,128)S(1)} %get-tuple-element.11.refs_2_), custom_call_target="tpu_custom_call" | custom-call | tf_op jit(solution)/shard_map/write_results/pallas_call | solution.py:578

commit v4 on v3

--- a/solution.py
+++ b/solution.py
@@ -14,6 +14,7 @@
 SUBLANES = 8
 SPLIT = 4
 UNROLL = 32
+JOINED = 2
 MESH = pl.DeviceIdType.MESH
 BOTH_LAST = (((1,), (1,)), ((), ()))
 
@@ -253,6 +254,11 @@
         return (away + seq_count - 1) // seq_count * frames + lax.rem(frame, frames)
 
     def run_block(resets, block, state):
+        for part in range(JOINED):
+            state = run_part(resets, block * JOINED + part, state)
+        return state
+
+    def run_part(resets, block, state):
         labels_v, blanks_v = state
         full = (labels_v, blanks_v, ones, ones)
         ahead_slot = history_slot(block * UNROLL)
@@ -266,8 +272,8 @@
         blanks_v = tuple(v + jnp.log2(x) for v, x in zip(blanks_v, blanks_x))
         return labels_v, blanks_v
 
-    blocks = steps // UNROLL
-    resetting = (steps // 2) // UNROLL
+    blocks = steps // (UNROLL * JOINED)
+    resetting = (steps // 2) // (UNROLL * JOINED)
     state = (tuple(label_start), tuple(blank_start))
     state = lax.fori_loop(0, resetting, functools.partial(run_block, True), state)
     lax.fori_loop(resetting, blocks, functools.partial(run_block, False), state)
@@ -276,8 +282,8 @@
     inner_frame = row // utterances
 
     def posterior_block(block, carry):
-        for pair in range(0, SUBLANES, 2):
-            low = block * SUBLANES + pair
+        for pair in range(0, 2 * SUBLANES, 2):
+            low = block * 2 * SUBLANES + pair
             first = pl.multiple_of(low * stored, rows)
 
             def ahead(index):
@@ -318,7 +324,7 @@
             mass_ref[pl.ds(pl.multiple_of(low * utterances, rows), rows), :] = mass * scale
         return carry
 
-    lax.fori_loop(0, frames // SUBLANES, posterior_block, 0)
+    lax.fori_loop(0, frames // (2 * SUBLANES), posterior_block, 0)
 
     times = start + lax.broadcasted_iota(jnp.int32, (frames, 1), 0)
     for u in range(utterances):

time: 41.7 us -> 40.5 us (0.971)
  Pallas kernels: 40.9 us -> 39.7 us
    pallas_call x1, Pallas kernels: 39.9 us -> 38.7 us  [shards(): pl.pallas_call(functools.partial(fused_kernel, seq_count, dp_count), out_...]
where the time goes in v4:
time: 40.5 us; the launch traced here: 40.3 us
  Pallas kernels  39.7 us (98%)
  between operations  0.64 us (2%)
    pallas_call x1, Pallas kernels, shards(): pl.pallas_call(functools.partial(fused_kernel, seq_count, dp_count), out_...  38.7 us
    pallas_call x1, Pallas kernels, shards(): pl.pallas_call(write_results, out_shape=(jax.ShapeDtypeStruct((utterances...  0.97 us

profile of v4, /device:TPU:0, one launch (start us, length us, event | category | flops | bytes accessed | tf_op | source)
XLA Modules:
  0.0 40.3 jit_solution(10946204321852064769)
XLA Ops:
  0.6 38.7 %fused.1 = (bf16[256,512]{1,0:T(8,128)(2,1)S(1)}, bf16[256,1280]{1,0:T(8,128)(2,1)S(1)}, f32[160,128]{1,0:T(8,128)S(1)}) custom-call(s32[4]{0:T(128)} %label_count_ref.1, s32[4]{0:T(128)} %frame_count_ref.1, bf16[256,1280]{1,0:T(8,128)(2,1)} %bitcast.3, bf16[1280,512]{1,0:T(8,128)(2,1)} %weight_ref.1, s32[4,63]{1,0:T(4,128)} %labels_ref.1), custom_call_target="tpu_custom_call" | custom-call | tf_op jit(solution)/shard_map/fused/pallas_call | solution.py:554
  39.4 1.0 %write_results.1 = (bf16[256,512]{1,0:T(8,128)(2,1)}, bf16[256,1280]{1,0:T(8,128)(2,1)}, f32[160,128]{1,0:T(8,128)}) custom-call(bf16[256,512]{1,0:T(8,128)(2,1)S(1)} %get-tuple-element.9.refs_0_, bf16[256,1280]{1,0:T(8,128)(2,1)S(1)} %get-tuple-element.10.refs_1_, f32[160,128]{1,0:T(8,128)S(1)} %get-tuple-element.11.refs_2_), custom_call_target="tpu_custom_call" | custom-call | tf_op jit(solution)/shard_map/write_results/pallas_call | solution.py:584

commit v5 on v4

--- a/solution.py
+++ b/solution.py
@@ -65,7 +65,7 @@
 
 
 def share_emissions(seq_count, enc_ref, weight_ref, labels_ref, prob_ref, gathered_ref, hot_ref,
-                    table_ref, send_sems, recv_sems, before_sending, meanwhile):
+                    table_ref, send_sems, recv_sems, before_sending, meanwhile, loads):
     utterances, length = labels_ref.shape
     me = lax.axis_index("seq")
     frames = enc_ref.shape[0] // utterances
@@ -74,7 +74,14 @@
     slots = length + 1
     own = pl.ds(pl.multiple_of(me * frames, frames), frames)
     character_tables(labels_ref, table_ref, hot_ref)
-    logits = jnp.dot(enc_ref[...], weight_ref[...], preferred_element_type=jnp.float32)
+    logits = None
+    half = weight_ref.shape[0] // 2
+    for part, pair in enumerate(loads):
+        for load in pair:
+            load.wait()
+        run = slice(part * half, (part + 1) * half)
+        product = jnp.dot(enc_ref[:, run], weight_ref[run, :], preferred_element_type=jnp.float32)
+        logits = product if logits is None else logits + product
     highest = jnp.max(logits, axis=1, keepdims=True)
     shifted = logits - highest
     powers = jnp.exp(shifted)
@@ -417,10 +424,20 @@
     return [(low, min(quarter, rows - low)) for low in range(0, rows, quarter)]
 
 
-def fused_kernel(seq_count, dp_count, label_count_ref, frame_count_ref, enc_ref, weight_ref,
+def fused_kernel(seq_count, dp_count, label_count_ref, frame_count_ref, enc_input, weight_input,
                  labels_ref, logit_ref, row_ref, out_ref, prob_ref, gathered_ref, hot_ref, table_ref,
                  turned_ref, ahead_ref, back_ref, mass_ref, sent_ref, kept_ref, share_send, share_recv,
-                 send_sems, recv_sems, *landed):
+                 send_sems, recv_sems, enc_ref, weight_ref, load_sems, *landed):
+    half = weight_ref.shape[0] // 2
+    loads = []
+    for part in range(2):
+        run = pl.ds(part * half, half)
+        loads.append((
+            pltpu.make_async_copy(weight_input.at[run], weight_ref.at[run], load_sems.at[part, 0]),
+            pltpu.make_async_copy(enc_input.at[:, run], enc_ref.at[:, run], load_sems.at[part, 1]),
+        ))
+        for load in loads[-1]:
+            load.start()
     me = lax.axis_index("seq")
     digits = {
         (axis, i): entry
@@ -440,7 +457,7 @@
         turned_ref[...] = jnp.transpose(enc_ref[...])
 
     share_emissions(seq_count, enc_ref, weight_ref, labels_ref, prob_ref, gathered_ref, hot_ref,
-                    table_ref, share_send, share_recv, before_sending, meanwhile)
+                    table_ref, share_send, share_recv, before_sending, meanwhile, loads)
     lattice_gradients(label_count_ref, frame_count_ref, gathered_ref, labels_ref, prob_ref, hot_ref,
                       logit_ref, table_ref, ahead_ref, back_ref, mass_ref)
 
@@ -558,7 +575,7 @@
             pltpu.VMEM((utterances * frames, width), jnp.bfloat16),
             pltpu.VMEM((block_rows, block_columns), jnp.float32),
         ),
-        in_specs=[smem, smem] + [vmem] * 3,
+        in_specs=[smem, smem] + [pl.BlockSpec(memory_space=pltpu.HBM)] * 2 + [vmem],
         out_specs=(vmem, vmem, vmem),
         scratch_shapes=[
             pltpu.VMEM((utterances * frames, vocabulary), jnp.float32),
@@ -575,6 +592,9 @@
             pltpu.SemaphoreType.DMA((seq_count - 1,)),
             pltpu.SemaphoreType.DMA((len(chunks),)),
             pltpu.SemaphoreType.DMA((len(chunks), len(held) + 1)),
+            pltpu.VMEM(flat_rows.shape, flat_rows.dtype),
+            pltpu.VMEM(out_weight.shape, out_weight.dtype),
+            pltpu.SemaphoreType.DMA((2, 2)),
         ] + landed,
         compiler_params=pltpu.CompilerParams(
             collective_id=0, has_side_effects=True, vmem_limit_bytes=60 * 1024 * 1024

time: 40.5 us -> 40.5 us (level)
  no operation moved by 1% of the time
where the time goes in v5:
time: 40.5 us; the launch traced here: 40.4 us
  Pallas kernels  39.7 us (98%)
  between operations  0.64 us (2%)
    pallas_call x1, Pallas kernels, shards(): pl.pallas_call(functools.partial(fused_kernel, seq_count, dp_count), out_...  38.8 us
    pallas_call x1, Pallas kernels, shards(): pl.pallas_call(write_results, out_shape=(jax.ShapeDtypeStruct((utterances...  0.97 us

profile of v5, /device:TPU:0, one launch (start us, length us, event | category | flops | bytes accessed | tf_op | source)
XLA Modules:
  0.0 40.4 jit_solution(5247206289276989338)
XLA Ops:
  0.6 38.8 %fused.1 = (bf16[256,512]{1,0:T(8,128)(2,1)S(1)}, bf16[256,1280]{1,0:T(8,128)(2,1)S(1)}, f32[160,128]{1,0:T(8,128)S(1)}) custom-call(s32[4]{0:T(128)} %label_count_ref.1, s32[4]{0:T(128)} %frame_count_ref.1, bf16[256,1280]{1,0:T(8,128)(2,1)} %bitcast.3, bf16[1280,512]{1,0:T(8,128)(2,1)} %weight_input.1, s32[4,63]{1,0:T(4,128)} %labels_ref.1), custom_call_target="tpu_custom_call" | custom-call | tf_op jit(solution)/shard_map/fused/pallas_call | solution.py:571
  39.4 1.0 %write_results.1 = (bf16[256,512]{1,0:T(8,128)(2,1)}, bf16[256,1280]{1,0:T(8,128)(2,1)}, f32[160,128]{1,0:T(8,128)}) custom-call(bf16[256,512]{1,0:T(8,128)(2,1)S(1)} %get-tuple-element.9.refs_0_, bf16[256,1280]{1,0:T(8,128)(2,1)S(1)} %get-tuple-element.10.refs_1_, f32[160,128]{1,0:T(8,128)S(1)} %get-tuple-element.11.refs_2_), custom_call_target="tpu_custom_call" | custom-call | tf_op jit(solution)/shard_map/write_results/pallas_call | solution.py:604
